TPU v7x, 32 devices: a whole 2x2x4 slice. The times are simulated.
32 devices in a mesh: width: 4 (over y, core), hidden: 8 (over z, x).
Axes of the slice: x: 2, y: 2, z: 4, core: 2. Of those that a mesh axis runs over, the one named last changes fastest.
Arguments:
- tokens: bfloat16 [1152, 5120], P(None, 'width'), may hold values from -6 to 6
- cotangent: bfloat16 [1152, 5120], P(None, 'width'), may hold values from -6 to 6
- w_up: bfloat16 [5120, 13824], P('width', 'hidden'), may hold values from -0.078125 to 0.078125
- bias_up: float32 [13824], P('hidden'), may hold values from -3 to 3
- w_down: bfloat16 [13824, 5120], P('hidden', 'width'), may hold values from -0.0546875 to 0.0546875
- mod_table: float32 [32, 3, 5120], P(None, None, 'width'), may hold values from -3 to 3
- seg_ids: int32 [1152], replicated, may hold values from 0 to 15, never falling along the last dimension, each value on 1 to 144 neighbouring positions
- step_ids: int32 [16], replicated, may hold values from 0 to 31
Outputs:
- grad_x: bfloat16 [1152, 5120], P(None, 'width')
- grad_up: float32 [5120, 13824], P('width', 'hidden')
- grad_down: float32 [13824, 5120], P('hidden', 'width')
- grad_bias: float32 [13824], P('hidden')
- grad_table: float32 [32, 3, 5120], P(None, None, 'width')
Inputs may be any that keep to these rules, and one draw needn't show every extreme that they name: `seg_ids`: request numbers never fall along the tokens and every request holds at least one token.
All inputs are finite; a program needn't handle non-finite values.
Results may differ from a plain program's by a relative error of at most 0.0063.
Values may be sent and summed in bfloat16 or wider, within the bound.
No kernel may reach another device: no remote copies, remote signals or barrier semaphores. Data moves between devices by JAX's collectives and lax.ppermute only.
A program may use at most 128 MiB of HBM per device.

v0:
```python
import jax
import jax.numpy as jnp
from jax import lax
from jax.sharding import PartitionSpec as P

D = 5120


def gelu_tanh(value):
    return jax.nn.gelu(value, approximate=True)


def norm_back(d_norm, x_hat, mod_gain, inv_std, cotangent):
    d_hat = d_norm * mod_gain
    feature_sums = lax.psum((jnp.sum(d_hat, 1), jnp.sum(d_hat * x_hat, 1)), "width")
    mean_one = feature_sums[0] / D
    mean_two = feature_sums[1] / D
    grad_rows = cotangent.astype(jnp.float32) + inv_std[:, None] * (
        d_hat - mean_one[:, None] - x_hat * mean_two[:, None]
    )
    return grad_rows.astype(jnp.bfloat16)


def per_device(tokens, cotangent, w_up, bias_up, w_down, mod_table, seg_ids, step_ids):
    highest = lax.Precision.HIGHEST
    req_count = step_ids.shape[0]
    table_rows = mod_table.shape[0]
    req_of = (seg_ids[:, None] == jnp.arange(req_count)[None, :]).astype(jnp.float32)
    step_of = (step_ids[:, None] == jnp.arange(table_rows)[None, :]).astype(jnp.float32)
    req_mod = jnp.einsum("rk,kcd->rcd", step_of, mod_table, precision=highest)
    shift_tok = jnp.dot(req_of, req_mod[:, 0], precision=highest)
    scale_tok = jnp.dot(req_of, req_mod[:, 1], precision=highest)
    gate_tok = jnp.dot(req_of, req_mod[:, 2], precision=highest)
    x_full = tokens.astype(jnp.float32)
    moment_one, moment_two = lax.psum((jnp.sum(x_full, 1), jnp.sum(x_full * x_full, 1)), "width")
    tok_mean = moment_one / D
    tok_var = moment_two / D - tok_mean * tok_mean
    inv_std = lax.rsqrt(tok_var + 1e-06)
    x_hat = (x_full - tok_mean[:, None]) * inv_std[:, None]
    mod_gain = 1.0 + scale_tok
    normed = (x_hat * mod_gain + shift_tok).astype(jnp.bfloat16)
    up_part = jnp.dot(normed, w_up, preferred_element_type=jnp.float32)
    pre_share = lax.psum_scatter(up_part, "width", scatter_dimension=0, tiled=True) + bias_up
    act_share = gelu_tanh(pre_share).astype(jnp.bfloat16)
    hidden_act = lax.all_gather(act_share, "width", axis=0, tiled=True)
    y_part = jnp.dot(hidden_act, w_down, preferred_element_type=jnp.float32)
    gate_part = jnp.dot(req_of.T, cotangent.astype(jnp.float32) * y_part, precision=highest)
    d_out = (cotangent.astype(jnp.float32) * gate_tok).astype(jnp.bfloat16)
    down_part = jnp.dot(d_out, w_down.T, preferred_element_type=jnp.float32)
    act_grad = lax.psum_scatter(down_part, "width", scatter_dimension=0, tiled=True)
    _, pull = jax.vjp(gelu_tanh, pre_share)
    pre_grad = pull(act_grad)[0]
    grad_bias = lax.psum(jnp.sum(pre_grad, 0), "width")
    d_pre_b = lax.all_gather(pre_grad.astype(jnp.bfloat16), "width", axis=0, tiled=True)
    grad_down = jnp.dot(hidden_act.T, d_out, preferred_element_type=jnp.float32)
    grad_up = jnp.dot(normed.T, d_pre_b, preferred_element_type=jnp.float32)
    d_part = jnp.dot(d_pre_b, w_up.T, preferred_element_type=jnp.float32)
    shift_part = jnp.dot(req_of.T, d_part, precision=highest)
    scale_part = jnp.dot(req_of.T, d_part * x_hat, precision=highest)
    req_grads = lax.psum(jnp.stack([shift_part, scale_part, gate_part], 1), "hidden")
    grad_table = jnp.einsum("rk,rcd->kcd", step_of, req_grads, precision=highest)
    d_norm = lax.psum(d_part, "hidden")
    grad_x = norm_back(d_norm, x_hat, mod_gain, inv_std, cotangent)
    return (grad_x, grad_up, grad_down, grad_bias, grad_table)


def solution(mesh):
    placed = (
        P(None, "width"),
        P(None, "width"),
        P("width", "hidden"),
        P("hidden"),
        P("hidden", "width"),
        P(None, None, "width"),
        P(),
        P(),
    )
    return jax.shard_map(
        per_device,
        mesh=mesh,
        in_specs=placed,
        out_specs=(
            P(None, "width"),
            P("width", "hidden"),
            P("hidden", "width"),
            P("hidden"),
            P(None, None, "width"),
        ),
        check_vma=False,
    )
```

profile of v0, /device:TPU:0, one launch (start us, length us, event | category | flops | bytes accessed | tf_op | source)
XLA Modules:
  0.0 515.7 jit_solution(15026594114937513184)
XLA Ops:
  7.2 0.0 copy-start
  7.2 0.0 copy-start.2
  7.2 0.0 copy-start.9
  7.2 0.0 reduce-scatter.5.cloned.1.call-start
  7.3 2.9 fusion.3
  10.1 12.7 %all-reduce.2 = (f32[1152]{0:T(1024)S(1)}, f32[1152]{0:T(1024)S(1)}) all-reduce(f32[1152]{0:T(1024)S(1)} %get-tuple-element.8, f32[1152]{0:T(1024)S(1)} %get-tuple-element.7), channel_id=1, replica_groups=mesh['width'=4,'hidden'=8] {'width'}, use_global_device_ids=true, to_apply=%region_3.0 | all-reduce | flops 2304 | bytes 18432 | tf_op jit(solution)/shard_map/psum | solution.py:35
  22.9 1.0 fusion.34
  23.9 0.0 copy-start.8
  23.9 0.0 slice-start
  23.9 3.4 convolution_add_fusion.1
  27.2 0.0 copy-start.3
  27.3 0.0 copy-done.8
  27.3 2.5 copy-done.3
  29.8 3.7 fusion.1
  33.5 0.0 copy-start.5
  33.6 1.6 copy-done.5
  35.2 7.7 %fusion.42 = f32[1152,1728]{1,0:T(8,128)} fusion(bf16[1152,1280]{1,0:T(8,128)(2,1)S(1)} %fusion.1, bf16[1280,1728]{0,1:T(8,128)(2,1)S(1)} %bitcast.36), kind=kOutput, calls=%fused_computation.59 | convolution fusion | flops 5096079360 | bytes 15335424 | tf_op jit(solution)/shard_map/dot_general | solution.py:42
  42.9 0.0 reduce-scatter.5.cloned.1.call-update
  42.9 0.0 reduce-scatter.3.cloned.1.call-start
  43.0 4.5 fusion
  47.5 1.7 copy-done.6
  49.1 10.2 %fusion.41 = f32[1152,1728]{1,0:T(8,128)} fusion(bf16[1152,1280]{1,0:T(8,128)(2,1)S(1)} %fusion, bf16[1728,1280]{1,0:T(8,128)(2,1)} %param.12), kind=kOutput, calls=%fused_computation.58 | convolution fusion | flops 5096079360 | bytes 15335424 | tf_op jit(solution)/shard_map/dot_general | solution.py:49
  59.4 0.0 reduce-scatter.3.cloned.1.call-update
  59.4 0.2 all-gather.3.cloned.1.call-start
  59.6 54.3 %reduce-scatter.5.cloned.1.call-done = f32[288,1728]{1,0:T(8,128)} async-done(((f32[1152,1728]{1,0:T(8,128)}), f32[288,1728]{1,0:T(8,128)}) %reduce-scatter.5.cloned.1.call-update) | async-done | bytes 1990672 | tf_op jit(solution)/shard_map/reduce_scatter | solution.py:43
  113.9 73.9 %reduce-scatter.3.cloned.1.call-done = f32[288,1728]{1,0:T(8,128)} async-done(((f32[1152,1728]{1,0:T(8,128)}), f32[288,1728]{1,0:T(8,128)}) %reduce-scatter.3.cloned.1.call-update) | async-done | bytes 1990672 | tf_op jit(solution)/shard_map/reduce_scatter | solution.py:50
  187.8 5.1 fusion.39
  192.9 0.0 all-gather.3.cloned.1.call-update
  193.0 0.0 all-gather.5.cloned.1.call-start
  193.0 0.5 all-gather.5.cloned.1.call-update
  193.5 0.0 all-reduce.5.cloned.1.call-start
  193.6 33.6 %all-gather.3.cloned.1.call-done = bf16[1152,1728]{1,0:T(8,128)(2,1)} async-done(((bf16[288,1728]{1,0:T(8,128)(2,1)}), bf16[1152,1728]{1,0:T(8,128)(2,1)}) %all-gather.3.cloned.1.call-update) | async-done | bytes 3981328 | tf_op jit(solution)/shard_map/all_gather | solution.py:54
  227.2 8.6 %fusion.43 = f32[1152,1280]{1,0:T(8,128)S(1)} fusion(bf16[1152,1728]{1,0:T(8,128)(2,1)} %all-gather.3.cloned.1.call-done, bf16[1280,1728]{0,1:T(8,128)(2,1)} %param.10), kind=kOutput, calls=%fused_computation.60 | convolution fusion | flops 5096079360 | bytes 14303232 | tf_op jit(solution)/shard_map/dot_general | solution.py:57
  235.8 2.1 convolution_bitcast_fusion.1
  237.9 0.8 copy-done.4
  238.7 2.8 fusion.16
  241.5 21.8 %all-gather.5.cloned.1.call-done = bf16[1152,1728]{1,0:T(8,128)(2,1)} async-done(((bf16[288,1728]{1,0:T(8,128)(2,1)}), bf16[1152,1728]{1,0:T(8,128)(2,1)}) %all-gather.5.cloned.1.call-update) | async-done | bytes 3981328 | tf_op jit(solution)/shard_map/all_gather | solution.py:45
  263.3 9.0 %convolution_multiply_fusion = f32[1152,1280]{1,0:T(8,128)S(1)} fusion(bf16[1152,1728]{1,0:T(8,128)(2,1)} %all-gather.5.cloned.1.call-done, bf16[1728,1280]{1,0:T(8,128)(2,1)} %param.12, bf16[1152,1280]{1,0:T(8,128)(2,1)} %param.9), kind=kOutput, calls=%fused_computation | convolution fusion | flops 5099028480 | bytes 17252352 | tf_op jit(solution)/shard_map/dot_general | solution.py:46
  272.4 2.1 convolution_bitcast_fusion
  274.5 0.7 pad_maximum_fusion
  275.2 0.0 all-reduce.5.cloned.1.call-update
  275.3 11.3 %fusion.44 = f32[1280,1728]{0,1:T(8,128)} fusion(bf16[1152,1280]{1,0:T(8,128)(2,1)} %copy-done.5, bf16[1152,1728]{1,0:T(8,128)(2,1)} %all-gather.3.cloned.1.call-done), kind=kOutput, calls=%fused_computation.61 | convolution fusion | flops 5096079360 | bytes 15777792 | tf_op jit(solution)/shard_map/dot_general | solution.py:56
  286.5 8.6 %fusion.45 = f32[1728,1280]{1,0:T(8,128)} fusion(bf16[1152,1728]{1,0:T(8,128)(2,1)S(1)} %copy-done.13, bf16[1152,1280]{1,0:T(8,128)(2,1)S(1)} %copy-done.7), kind=kOutput, calls=%fused_computation.62 | convolution fusion | flops 5096079360 | bytes 15777792 | tf_op jit(solution)/shard_map/dot_general | solution.py:55
  295.1 187.8 %all-reduce.5.cloned.1.call-done = (f32[1152,1280]{1,0:T(8,128)}, f32[16,3,1280]{2,0,1:T(8,128)}) async-done(((f32[1152,1280]{1,0:T(8,128)}, f32[16,3,1280]{2,0,1:T(8,128)}), (f32[1152,1280]{1,0:T(8,128)}, f32[16,3,1280]{2,0,1:T(8,128)})) %all-reduce.5.cloned.1.call-update) | async-done | bytes 6144016 | tf_op jit(solution)/shard_map/psum | solution.py:62
  482.9 8.0 %fusion.38 = (f32[1152]{0:T(1024)S(1)}, f32[1152]{0:T(1024)S(1)}, f32[1152,1280]{1,0:T(8,128)}) fusion(f32[1152]{0:T(1024)S(1)} %get-tuple-element.21, f32[1152]{0:T(1024)S(1)} %get-tuple-element.20, bf16[1152,1280]{1,0:T(8,128)(2,1)S(1)} %copy-done.2, f32[1152,1280]{1,0:T(8,128)} %get-tuple-element.9, f32[1152,1280]{1,0:T(8,128)} %copy-done.3), kind=kLoop, calls=%fused_computation.56 | loop fusion | flops 10319616 | bytes 20662272 | tf_op jit(solution)/shard_map/reduce_sum | solution.py:15
  490.8 1.3 fusion.32
  492.1 11.2 %all-reduce.1 = (f32[1152]{0:T(1024)S(1)}, f32[1152]{0:T(1024)S(1)}, f32[1728]{0:T(1024)}) all-reduce(f32[1152]{0:T(1024)S(1)} %get-tuple-element.6, f32[1152]{0:T(1024)S(1)} %get-tuple-element.5, f32[1728]{0:T(1024)S(1)} %get-tuple-element.16), channel_id=1, replica_groups=mesh['width'=4,'hidden'=8] {'width'}, use_global_device_ids=true, to_apply=%region_10.0 | all-reduce | flops 4032 | bytes 32256 | tf_op jit(solution)/shard_map/psum | solution.py:15
  503.3 5.9 %fusion.2 = bf16[1152,1280]{1,0:T(8,128)(2,1)} fusion(bf16[1152,1280]{1,0:T(8,128)(2,1)} %param.9, bf16[1152,1280]{1,0:T(8,128)(2,1)S(1)} %copy-done.2, f32[1152,1280]{1,0:T(8,128)} %get-tuple-element.18, f32[1152]{0:T(1024)S(1)} %get-tuple-element.22, f32[1152]{0:T(1024)S(1)} %get-tuple-element.23, f32[1152]{0:T(1024)S(1)} %get-tuple-element.20, ...), kind=kLoop, calls=%fused_computation.10 | loop fusion | flops 14745600 | bytes 14764032 | tf_op jit(solution)/shard_map/convert_element_type | solution.py:21
  (23 shorter events, 0.1 us)
Async XLA Ops:
  7.2 15.7 %copy-start = (f32[32,3,1280]{2,0,1:T(8,128)S(1)}, f32[32,3,1280]{2,0,1:T(8,128)}, u32[]{:S(2)}) copy-start(f32[32,3,1280]{2,0,1:T(8,128)} %param.13) | copy-start | bytes 1474564
  7.2 22.6 %copy-start.2 = (bf16[1152,1280]{1,0:T(8,128)(2,1)S(1)}, bf16[1152,1280]{1,0:T(8,128)(2,1)}, u32[]{:S(2)}) copy-start(bf16[1152,1280]{1,0:T(8,128)(2,1)} %param.8) | copy-start | bytes 8847364
  7.2 22.6 %copy-start.9 = (s32[1152]{0:T(1024)S(1)}, s32[1152]{0:T(1024)}, u32[]{:S(2)}) copy-start(s32[1152]{0:T(1024)} %param.14) | copy-start | bytes 13828
  7.2 106.7 %reduce-scatter.5.cloned.1.call-start = ((), (), s32[]{:S(2)}) async-start(), calls=%async_computation.3 | async-start | bytes 10321920 | tf_op jit(solution)/shard_map/reduce_scatter | solution.py:43
  23.9 3.4 copy-start.8
  23.9 11.3 %slice-start = ((s8[4423680]{0:T(1024)(128)(4,1)}), s8[4194304]{0:T(1024)(128)(4,1)S(1)}, s32[]{:S(2)}) async-start(s8[4423680]{0:T(1024)(128)(4,1)} %bitcast.35), calls=%async_computation.7 | async-start | bytes 8388608
  27.2 2.5 copy-start.3
  29.8 5.4 %slice-start.1 = ((s8[4423680]{0:T(1024)(128)(4,1)}), s8[229376]{0:T(1024)(128)(4,1)S(1)}, s32[]{:S(2)}) async-start(s8[4423680]{0:T(1024)(128)(4,1)} %bitcast.35), calls=%async_computation.8 | async-start | bytes 458752
  33.5 1.6 copy-start.5
  42.9 144.9 %reduce-scatter.3.cloned.1.call-start = ((), (), s32[]{:S(2)}) async-start(), calls=%async_computation.2 | async-start | bytes 10321920 | tf_op jit(solution)/shard_map/reduce_scatter | solution.py:50
  47.4 1.7 copy-start.6
  59.4 128.5 %copy-start.11 = (f32[1728]{0:T(1024)S(1)}, f32[1728]{0:T(1024)}, u32[]{:S(2)}) copy-start(f32[1728]{0:T(1024)} %param.11) | copy-start | bytes 20740
  59.4 167.8 %all-gather.3.cloned.1.call-start = ((), (), s32[]{:S(2)}) async-start(), calls=%async_computation.4 | async-start | bytes 5160960 | tf_op jit(solution)/shard_map/all_gather | solution.py:54
  193.0 70.4 %all-gather.5.cloned.1.call-start = ((), (), s32[]{:S(2)}) async-start(), calls=%async_computation.5 | async-start | bytes 5160960 | tf_op jit(solution)/shard_map/all_gather | solution.py:45
  193.5 289.3 %all-reduce.5.cloned.1.call-start = ((), (), s32[]{:S(2)}) async-start(), calls=%async_computation.6 | async-start | bytes 12288000 | tf_op jit(solution)/shard_map/psum | solution.py:62
  235.8 2.9 copy-start.4
  275.3 11.3 %copy-start.7 = (bf16[1152,1280]{1,0:T(8,128)(2,1)S(1)}, bf16[1152,1280]{1,0:T(8,128)(2,1)}, u32[]{:S(2)}) copy-start(bf16[1152,1280]{1,0:T(8,128)(2,1)} %copy-done.6) | copy-start | bytes 8847364
  275.3 11.3 %copy-start.13 = (bf16[1152,1728]{1,0:T(8,128)(2,1)S(1)}, bf16[1152,1728]{1,0:T(8,128)(2,1)}, u32[]{:S(2)}) copy-start(bf16[1152,1728]{1,0:T(8,128)(2,1)} %all-gather.5.cloned.1.call-done) | copy-start | bytes 11943940
  482.9 8.0 %copy-start.10 = (f32[16,3,1280]{2,0,1:T(8,128)S(1)}, f32[16,3,1280]{2,0,1:T(8,128)}, u32[]{:S(2)}) copy-start(f32[16,3,1280]{2,0,1:T(8,128)} %get-tuple-element.10) | copy-start | bytes 737284
  482.9 8.0 %copy-start.12 = (s32[16]{0:T(128)S(1)}, s32[16]{0:T(128)}, u32[]{:S(2)}) copy-start(s32[16]{0:T(128)} %param.15) | copy-start | bytes 196
  503.3 5.9 %copy-start.1 = (f32[32,3,1280]{2,0,1:T(8,128)S(1)}, f32[32,3,1280]{2,0,1:T(8,128)}, u32[]{:S(2)}) copy-start(f32[32,3,1280]{2,0,1:T(8,128)} %param.13) | copy-start | bytes 1474564
Sparse Core Ops, SparseCore 0:
  43.0 70.8 reduce-scatter.4
  117.2 70.6 reduce-scatter.2
  193.1 34.0 all-gather.2
  229.2 34.0 all-gather.4
  275.4 207.4 all-reduce.4
where the time goes:
time: 516 us
  waiting for transfers between devices  372 us (72%)
  matrix products  76.3 us (15%)
  blocking collectives  23.9 us (5%)
  other arithmetic  22.6 us (4%)
  between operations  13.9 us (3%)
  local copies, waits for them, and re-layouts  6.61 us (1%)
    psum x1, waiting for transfers between devices, per_device(): d_norm = lax.psum(d_part, 'hidden')  188 us
    reduce_scatter x1, waiting for transfers between devices, per_device(): lax.psum_scatter(down_part, 'width', scatter_dimension=0, tiled=True)  73.9 us
    reduce_scatter x1, waiting for transfers between devices, per_device(): lax.psum_scatter(up_part, 'width', scatter_dimension=0, tiled=True)  54.3 us
    all_gather x1, waiting for transfers between devices, per_device(): lax.all_gather(pre_grad.astype(jnp.bfloat16), 'width', axis=0, tiled=True)  33.6 us
    all_gather x1, waiting for transfers between devices, per_device(): hidden_act = lax.all_gather(act_share, 'width', axis=0, tiled=True)  21.8 us
    psum x1, blocking collectives, per_device(): lax.psum((jnp.sum(x_full, 1), jnp.sum(x_full * x_full, 1)), 'width')  12.7 us
    dot_general x1, matrix products, per_device(): grad_up = jnp.dot(normed.T, d_pre_b, preferred_element_type=jnp.float32)  11.3 us
    psum x1, blocking collectives, norm_back(): lax.psum((jnp.sum(d_hat, 1), jnp.sum(d_hat * x_hat, 1)), 'width')  11.2 us
  transfers between devices with their start and end apart: 5, of which 5 were waited for; matrix products, arithmetic and copies ran while one was open for 9% of the time, Pallas kernels for 0%

commit v1 on v0

--- a/solution.py
+++ b/solution.py
@@ -59,7 +59,9 @@
     scale_part = jnp.dot(req_of.T, d_part * x_hat, precision=highest)
     req_grads = lax.psum(jnp.stack([shift_part, scale_part, gate_part], 1), "hidden")
     grad_table = jnp.einsum("rk,rcd->kcd", step_of, req_grads, precision=highest)
-    d_norm = lax.psum(d_part, "hidden")
+    d_norm = d_part
+    for hop in (1, 2, 4):
+        d_norm = d_norm + lax.ppermute(d_norm, "hidden", [(dev, dev ^ hop) for dev in range(8)])
     grad_x = norm_back(d_norm, x_hat, mod_gain, inv_std, cotangent)
     return (grad_x, grad_up, grad_down, grad_bias, grad_table)
 

time: 516 us -> 862 us (1.67); the launches traced: 516 us -> 853 us
  waiting for transfers between devices: 372 us -> 686 us
  other arithmetic: 22.6 us -> 34.9 us
    ppermute x0 -> x3, waiting for transfers between devices: none -> 255 us  [per_device(): lax.ppermute(d_norm, 'hidden', [(dev, dev ^ hop) for dev in range(8)])]
    psum x1, waiting for transfers between devices: 188 us -> 268 us  [per_device(): lax.psum(jnp.stack([shift_part, scale_part, gate_part], 1), 'hidden')]
    all_gather x1, waiting for transfers between devices: 21.8 us -> 0.02 us  [per_device(): hidden_act = lax.all_gather(act_share, 'width', axis=0, tiled=True)]
    add x0 -> x2, other arithmetic: none -> 10.9 us  [per_device(): d_norm + lax.ppermute(d_norm, 'hidden', [(dev, dev ^ hop) for dev in rang...]
  transfers between devices with their start and end apart: 5 -> 8, of which waited for: 5 -> 6; matrix products, arithmetic and copies ran while one was open for 9% -> 8% of each run, Pallas kernels for 0% -> 0%
where the time goes in v1:
time: 862 us; the launch traced here: 853 us
  waiting for transfers between devices  686 us (80%)
  matrix products  82.9 us (10%)
  other arithmetic  34.9 us (4%)
  blocking collectives  23.6 us (3%)
  between operations  14.2 us (2%)
    psum x1, waiting for transfers between devices, per_device(): lax.psum(jnp.stack([shift_part, scale_part, gate_part], 1), 'hidden')  268 us
    ppermute x3, waiting for transfers between devices, per_device(): lax.ppermute(d_norm, 'hidden', [(dev, dev ^ hop) for dev in range(8)])  255 us
    reduce_scatter x1, waiting for transfers between devices, per_device(): lax.psum_scatter(down_part, 'width', scatter_dimension=0, tiled=True)  73.8 us
    reduce_scatter x1, waiting for transfers between devices, per_device(): lax.psum_scatter(up_part, 'width', scatter_dimension=0, tiled=True)  54.3 us
    all_gather x1, waiting for transfers between devices, per_device(): lax.all_gather(pre_grad.astype(jnp.bfloat16), 'width', axis=0, tiled=True)  34.2 us
  transfers between devices with their start and end apart: 8, of which 6 were waited for; matrix products, arithmetic and copies ran while one was open for 8% of the time, Pallas kernels for 0%

profile of v1, /device:TPU:0, one launch (start us, length us, event | category | flops | bytes accessed | tf_op | source)
XLA Modules:
  0.0 853.0 jit_solution(11700602227299730101)
XLA Ops:
  7.2 0.0 copy-start
  7.2 0.0 reduce-scatter.5.cloned.1.call-start
  7.3 2.9 fusion.3
  10.1 12.7 %all-reduce.1 = (f32[1152]{0:T(1024)S(1)}, f32[1152]{0:T(1024)S(1)}) all-reduce(f32[1152]{0:T(1024)S(1)} %get-tuple-element.8, f32[1152]{0:T(1024)S(1)} %get-tuple-element.7), channel_id=1, replica_groups=mesh['width'=4,'hidden'=8] {'width'}, use_global_device_ids=true, to_apply=%region_3.0 | all-reduce | flops 2304 | bytes 18432 | tf_op jit(solution)/shard_map/psum | solution.py:35
  22.9 1.0 fusion.34
  23.9 0.0 slice-start
  23.9 3.4 convolution_add_fusion.1
  27.3 2.5 copy-done.3
  29.8 3.7 fusion.1
  33.5 1.6 copy-done.5
  35.1 7.7 fusion.42
  42.9 0.0 reduce-scatter.5.cloned.1.call-update
  42.9 0.0 reduce-scatter.3.cloned.1.call-start
  42.9 4.5 fusion
  47.4 1.7 copy-done.6
  49.1 10.2 %fusion.41 = f32[1152,1728]{1,0:T(8,128)} fusion(bf16[1152,1280]{1,0:T(8,128)(2,1)S(1)} %fusion, bf16[1728,1280]{1,0:T(8,128)(2,1)} %param.12), kind=kOutput, calls=%fused_computation.59 | convolution fusion | flops 5096079360 | bytes 15335424 | tf_op jit(solution)/shard_map/dot_general | solution.py:49
  59.3 0.0 reduce-scatter.3.cloned.1.call-update
  59.3 0.3 all-gather.3.cloned.1.call-start
  59.6 54.3 %reduce-scatter.5.cloned.1.call-done = f32[288,1728]{1,0:T(8,128)} async-done(((f32[1152,1728]{1,0:T(8,128)}), f32[288,1728]{1,0:T(8,128)}) %reduce-scatter.5.cloned.1.call-update) | async-done | bytes 1990672 | tf_op jit(solution)/shard_map/reduce_scatter | solution.py:43
  113.9 73.8 %reduce-scatter.3.cloned.1.call-done = f32[288,1728]{1,0:T(8,128)} async-done(((f32[1152,1728]{1,0:T(8,128)}), f32[288,1728]{1,0:T(8,128)}) %reduce-scatter.3.cloned.1.call-update) | async-done | bytes 1990672 | tf_op jit(solution)/shard_map/reduce_scatter | solution.py:50
  187.8 5.1 fusion.39
  192.9 0.0 all-gather.3.cloned.1.call-update
  192.9 0.0 all-gather.5.cloned.1.call-start
  193.0 34.2 %all-gather.3.cloned.1.call-done = bf16[1152,1728]{1,0:T(8,128)(2,1)} async-done(((bf16[288,1728]{1,0:T(8,128)(2,1)}), bf16[1152,1728]{1,0:T(8,128)(2,1)}) %all-gather.3.cloned.1.call-update) | async-done | bytes 3981328 | tf_op jit(solution)/shard_map/all_gather | solution.py:54
  227.2 8.6 %fusion.43 = f32[1152,1280]{1,0:T(8,128)S(1)} fusion(bf16[1152,1728]{1,0:T(8,128)(2,1)} %all-gather.3.cloned.1.call-done, bf16[1280,1728]{0,1:T(8,128)(2,1)} %param.10), kind=kOutput, calls=%fused_computation.61 | convolution fusion | flops 5096079360 | bytes 14303232 | tf_op jit(solution)/shard_map/dot_general | solution.py:57
  235.8 1.5 collective-permute-start
  237.3 127.8 %collective-permute-done = f32[1152,1280]{1,0:T(8,128)S(1)} collective-permute-done((f32[1152,1280]{1,0:T(8,128)S(1)}, f32[1152,1280]{1,0:T(8,128)S(1)}, u32[]{:S(2)}, u32[]{:S(2)}) %collective-permute-start) | collective-permute-done | bytes 5898272 | tf_op jit(solution)/shard_map/ppermute | solution.py:64
  365.1 3.3 add.69
  368.4 1.5 collective-permute-start.1
  369.8 0.0 all-gather.5.cloned.1.call-update
  369.9 0.0 all-reduce.4.cloned.1.call-start
  369.9 127.1 %collective-permute-done.1 = f32[1152,1280]{1,0:T(8,128)} collective-permute-done((f32[1152,1280]{1,0:T(8,128)}, f32[1152,1280]{1,0:T(8,128)}, u32[]{:S(2)}, u32[]{:S(2)}) %collective-permute-start.1) | collective-permute-done | bytes 5898272 | tf_op jit(solution)/shard_map/ppermute | solution.py:64
  497.0 7.6 add.70
  504.7 2.4 collective-permute-start.2
  507.1 4.7 convolution_bitcast_fusion.1
  511.8 0.0 all-gather.5.cloned.1.call-done
  511.9 9.5 %convolution_multiply_fusion = f32[1152,1280]{1,0:T(8,128)S(1)} fusion(bf16[1152,1728]{1,0:T(8,128)(2,1)} %all-gather.5.cloned.1.call-done, bf16[1728,1280]{1,0:T(8,128)(2,1)} %param.12, bf16[1152,1280]{1,0:T(8,128)(2,1)} %param.9), kind=kOutput, calls=%fused_computation | convolution fusion | flops 5099028480 | bytes 17252352 | tf_op jit(solution)/shard_map/dot_general | solution.py:46
  521.4 2.1 convolution_bitcast_fusion
  523.5 5.5 fusion.16
  529.0 0.7 pad_maximum_fusion
  529.7 0.0 all-reduce.4.cloned.1.call-update
  529.8 11.0 %fusion.44 = f32[1280,1728]{0,1:T(8,128)} fusion(bf16[1152,1280]{1,0:T(8,128)(2,1)} %copy-done.5, bf16[1152,1728]{1,0:T(8,128)(2,1)} %all-gather.3.cloned.1.call-done), kind=kOutput, calls=%fused_computation.62 | convolution fusion | flops 5096079360 | bytes 15777792 | tf_op jit(solution)/shard_map/dot_general | solution.py:56
  540.8 8.7 %fusion.45 = f32[1728,1280]{1,0:T(8,128)} fusion(bf16[1152,1728]{1,0:T(8,128)(2,1)S(1)} %copy-done.12, bf16[1152,1280]{1,0:T(8,128)(2,1)S(1)} %copy-done.7), kind=kOutput, calls=%fused_computation.63 | convolution fusion | flops 5096079360 | bytes 15777792 | tf_op jit(solution)/shard_map/dot_general | solution.py:55
  549.6 268.4 %all-reduce.4.cloned.1.call-done = f32[16,3,1280]{2,0,1:T(8,128)} async-done(((f32[16,3,1280]{2,0,1:T(8,128)}), f32[16,3,1280]{2,0,1:T(8,128)}) %all-reduce.4.cloned.1.call-update) | async-done | bytes 245776 | tf_op jit(solution)/shard_map/psum | solution.py:60
  818.0 2.2 fusion.32
  820.2 9.4 %fusion.38 = (f32[1152]{0:T(1024)S(1)}, f32[1152]{0:T(1024)S(1)}, f32[1152,1280]{1,0:T(8,128)}) fusion(f32[1152]{0:T(1024)S(1)} %get-tuple-element.19, f32[1152]{0:T(1024)S(1)} %get-tuple-element.18, bf16[1152,1280]{1,0:T(8,128)(2,1)S(1)} %copy-done.2, f32[1152,1280]{1,0:T(8,128)} %copy-done.3, f32[1152,1280]{1,0:T(8,128)} %add.70, ...), kind=kLoop, calls=%fused_computation.57 | loop fusion | flops 11794176 | bytes 26560512 | tf_op jit(solution)/shard_map/reduce_sum | solution.py:15
  829.6 10.8 %all-reduce = (f32[1152]{0:T(1024)S(1)}, f32[1152]{0:T(1024)S(1)}, f32[1728]{0:T(1024)}) all-reduce(f32[1152]{0:T(1024)S(1)} %get-tuple-element.6, f32[1152]{0:T(1024)S(1)} %get-tuple-element.5, f32[1728]{0:T(1024)S(1)} %get-tuple-element.14), channel_id=1, replica_groups=mesh['width'=4,'hidden'=8] {'width'}, use_global_device_ids=true, to_apply=%region_9.0 | all-reduce | flops 4032 | bytes 32256 | tf_op jit(solution)/shard_map/psum | solution.py:15
  840.4 5.9 fusion.2
  (29 shorter events, 0.1 us)
Async XLA Ops:
  7.2 15.7 %copy-start = (f32[32,3,1280]{2,0,1:T(8,128)S(1)}, f32[32,3,1280]{2,0,1:T(8,128)}, u32[]{:S(2)}) copy-start(f32[32,3,1280]{2,0,1:T(8,128)} %param.13) | copy-start | bytes 1474564
  7.2 22.6 %copy-start.2 = (bf16[1152,1280]{1,0:T(8,128)(2,1)S(1)}, bf16[1152,1280]{1,0:T(8,128)(2,1)}, u32[]{:S(2)}) copy-start(bf16[1152,1280]{1,0:T(8,128)(2,1)} %param.8) | copy-start | bytes 8847364
  7.2 22.6 %copy-start.9 = (s32[1152]{0:T(1024)S(1)}, s32[1152]{0:T(1024)}, u32[]{:S(2)}) copy-start(s32[1152]{0:T(1024)} %param.14) | copy-start | bytes 13828
  7.2 106.7 %reduce-scatter.5.cloned.1.call-start = ((), (), s32[]{:S(2)}) async-start(), calls=%async_computation.3 | async-start | bytes 10321920 | tf_op jit(solution)/shard_map/reduce_scatter | solution.py:43
  23.9 3.4 copy-start.8
  23.9 11.3 %slice-start = ((s8[4423680]{0:T(1024)(128)(4,1)}), s8[4194304]{0:T(1024)(128)(4,1)S(1)}, s32[]{:S(2)}) async-start(s8[4423680]{0:T(1024)(128)(4,1)} %bitcast.35), calls=%async_computation.7 | async-start | bytes 8388608
  27.2 2.5 copy-start.3
  29.8 5.4 slice-start.1
  33.5 1.6 copy-start.5
  42.9 144.9 %reduce-scatter.3.cloned.1.call-start = ((), (), s32[]{:S(2)}) async-start(), calls=%async_computation.2 | async-start | bytes 10321920 | tf_op jit(solution)/shard_map/reduce_scatter | solution.py:50
  47.4 1.7 copy-start.6
  59.3 128.5 %copy-start.10 = (f32[1728]{0:T(1024)S(1)}, f32[1728]{0:T(1024)}, u32[]{:S(2)}) copy-start(f32[1728]{0:T(1024)} %param.11) | copy-start | bytes 20740
  59.3 167.8 %all-gather.3.cloned.1.call-start = ((), (), s32[]{:S(2)}) async-start(), calls=%async_computation.4 | async-start | bytes 5160960 | tf_op jit(solution)/shard_map/all_gather | solution.py:54
  192.9 318.9 %all-gather.5.cloned.1.call-start = ((), (), s32[]{:S(2)}) async-start(), calls=%async_computation.5 | async-start | bytes 5160960 | tf_op jit(solution)/shard_map/all_gather | solution.py:45
  235.8 132.6 %copy-start.4 = (f32[1152,1280]{1,0:T(8,128)}, f32[1152,1280]{1,0:T(8,128)S(1)}, u32[]{:S(2)}) copy-start(f32[1152,1280]{1,0:T(8,128)S(1)} %fusion.43) | copy-start | bytes 17694724
  235.8 129.3 %collective-permute-start = (f32[1152,1280]{1,0:T(8,128)S(1)}, f32[1152,1280]{1,0:T(8,128)S(1)}, u32[]{:S(2)}, u32[]{:S(2)}) collective-permute-start(f32[1152,1280]{1,0:T(8,128)S(1)} %fusion.43), channel_id=1, source_target_pairs={{0,1},{1,0},{2,3},{3,2},{4,5},{5,4},{6,7},{7,6},{8,9},{9,8},{10,11... | collective-permute-start | bytes 17694728 | tf_op jit(solution)/shard_map/ppermute | solution.py:64
  368.4 128.7 %collective-permute-start.1 = (f32[1152,1280]{1,0:T(8,128)}, f32[1152,1280]{1,0:T(8,128)}, u32[]{:S(2)}, u32[]{:S(2)}) collective-permute-start(f32[1152,1280]{1,0:T(8,128)} %add.69), channel_id=1, source_target_pairs={{0,2},{1,3},{2,0},{3,1},{4,6},{5,7},{6,4},{7,5},{8,10},{9,11},{10,... | collective-permute-start | bytes 17694728 | tf_op jit(solution)/shard_map/ppermute | solution.py:64
  369.9 448.1 %all-reduce.4.cloned.1.call-start = ((), (), s32[]{:S(2)}) async-start(), calls=%async_computation.6 | async-start | bytes 491520 | tf_op jit(solution)/shard_map/psum | solution.py:60
  504.7 315.5 %collective-permute-start.2 = (f32[1152,1280]{1,0:T(8,128)}, f32[1152,1280]{1,0:T(8,128)}, u32[]{:S(2)}, u32[]{:S(2)}) collective-permute-start(f32[1152,1280]{1,0:T(8,128)} %add.70), channel_id=1, source_target_pairs={{0,4},{1,5},{2,6},{3,7},{4,0},{5,1},{6,2},{7,3},{8,12},{9,13},{10,... | collective-permute-start | bytes 17694728 | tf_op jit(solution)/shard_map/ppermute | solution.py:64
  529.7 11.1 %copy-start.7 = (bf16[1152,1280]{1,0:T(8,128)(2,1)S(1)}, bf16[1152,1280]{1,0:T(8,128)(2,1)}, u32[]{:S(2)}) copy-start(bf16[1152,1280]{1,0:T(8,128)(2,1)} %copy-done.6) | copy-start | bytes 8847364
  529.7 11.1 %copy-start.12 = (bf16[1152,1728]{1,0:T(8,128)(2,1)S(1)}, bf16[1152,1728]{1,0:T(8,128)(2,1)}, u32[]{:S(2)}) copy-start(bf16[1152,1728]{1,0:T(8,128)(2,1)} %all-gather.5.cloned.1.call-done) | copy-start | bytes 11943940
  540.8 277.2 %copy-start.11 = (s32[16]{0:T(128)S(1)}, s32[16]{0:T(128)}, u32[]{:S(2)}) copy-start(s32[16]{0:T(128)} %param.15) | copy-start | bytes 196
  840.4 5.9 copy-start.1
Sparse Core Ops, SparseCore 0:
  43.0 70.8 reduce-scatter.4
  117.2 70.5 reduce-scatter.2
  193.1 34.0 all-gather.2
  370.0 33.1 all-gather.4
  529.9 288.0 all-reduce.3
